TPU v7x, 128 devices: a whole 4x4x4 slice. The times are simulated.
128 devices in a mesh: req: 8 (over y, z_hi), mlp: 16 (over z_lo, x, core).
Axes of the slice: x: 4, y: 4, z: 4 (z_hi: 2, z_lo: 2; z = z_hi * 2 + z_lo), core: 2. Of those that a mesh axis runs over, the one named last changes fastest.
Arguments:
- prompt_tokens: bfloat16 [16, 1024, 2048], P('req', None, 'mlp'), may hold values from -6 to 6
- decode_tokens: bfloat16 [32, 2048], P('req', 'mlp'), may hold values from -6 to 6
- prompt_lengths: int32 [16], P('req'), may hold values from 128 to 1024, as said below
- decode_states: float32 [32, 16, 128, 128], P('req', 'mlp'), may hold values from -6 to 6
- w_fio: float32 [2048, 6144], P('req', 'mlp'), may hold values from -0.125 to 0.125
- forget_bias: float32 [2048], P('mlp'), as said below
- head_gain: float32 [2048], P('mlp'), may hold values from 0.1 to 1.9
- w_out: float32 [2048, 2048], P('mlp', 'req'), may hold values from -0.125 to 0.125
- mlp_gain: float32 [2048], replicated, may hold values from 0.1 to 1.9
- w_gu: float32 [2048, 11264], P('req', 'mlp'), may hold values from -0.125 to 0.125
- w_down: float32 [5632, 2048], P('mlp', 'req'), may hold values from -0.078125 to 0.078125
Outputs:
- prompt_out: bfloat16 [16, 1024, 2048], P('req', None, 'mlp')
- decode_out: bfloat16 [32, 2048], P('req', 'mlp')
- prompt_states: float32 [16, 16, 128, 128], P('req', 'mlp')
- decode_next: float32 [32, 16, 128, 128], P('req', 'mlp')
Inputs may be any that keep to these rules, and one draw needn't show every extreme that they name: `prompt_lengths`: slots at or past a prompt's length are padding; one prompt has length 1024 and another 1024 // 8. `forget_bias`: every entry is at least 3 and at most ln(1024) + 1.7.
All inputs are finite; a program needn't handle non-finite values.
Results may differ from a plain program's by a relative error of at most 0.02.
Values may be sent and summed in bfloat16 or wider, within the bound.
No kernel may reach another device: no remote copies, remote signals or barrier semaphores. Data moves between devices by JAX's collectives and lax.ppermute only.
A program may use at most 128 MiB of HBM per device.

v0:
```python
import jax
import jax.numpy as jnp
from jax import lax
from jax.sharding import PartitionSpec as P

BLOCK = 64
epsilon = 1e-05


def add_columns(operand, weights_piece):
    return jnp.dot(operand, weights_piece, preferred_element_type=jnp.float32)


def project_output(source_rows, weights):
    return jnp.dot(
        source_rows,
        lax.all_gather(weights, "req", axis=1, tiled=True),
        preferred_element_type=jnp.float32,
    )


def block_step(carried, forget_block, value_block, query_block, start_row, lengths):
    steps_here = forget_block.shape[1]
    positions = start_row + jnp.arange(steps_here, dtype=jnp.int32)
    alive_mask = (positions[None, :] < lengths[:, None])[:, :, None, None]
    log_forget = jnp.where(alive_mask, jax.nn.log_sigmoid(forget_block), 0.0)
    key_gate = jnp.where(alive_mask, jax.nn.sigmoid(-forget_block), 0.0)
    cumulated = jnp.cumsum(log_forget, axis=1)
    query_tilde = query_block * jnp.exp(cumulated)
    key_tilde = key_gate * jnp.exp(-cumulated)
    scores = jnp.einsum("pthc,pshc->phts", query_tilde, key_tilde, precision=lax.Precision.HIGHEST)
    triangle = jnp.arange(steps_here)[:, None] >= jnp.arange(steps_here)[None, :]
    scores = jnp.where(triangle, scores, 0.0)
    emitted = jnp.einsum("phts,pshv->pthv", scores, value_block, precision=lax.Precision.HIGHEST)
    emitted = emitted + jnp.einsum(
        "pthc,phcv->pthv", query_tilde, carried, precision=lax.Precision.HIGHEST
    )
    emitted = jnp.where(alive_mask, emitted, 0.0)
    last_log = cumulated[:, -1]
    key_decayed = key_gate * jnp.exp(last_log[:, None] - cumulated)
    carried = jnp.exp(last_log)[..., None] * carried + jnp.einsum(
        "pthc,pthv->phcv", key_decayed, value_block, precision=lax.Precision.HIGHEST
    )
    return (carried, emitted)


def on_device(
    prompt_tokens,
    decode_tokens,
    prompt_lengths,
    decode_states,
    w_fio,
    forget_bias,
    head_gain,
    w_out,
    mlp_gain,
    w_gu,
    w_down,
):
    prompts_here, plen, feature_part = prompt_tokens.shape
    heads_here = decode_states.shape[1]
    head_size = decode_states.shape[2]
    prompt_rows = prompts_here * plen
    local_rows = jnp.concatenate(
        [prompt_tokens.reshape(prompt_rows, feature_part), decode_tokens], axis=0
    )
    row_count = local_rows.shape[0]
    x_full = lax.all_gather(local_rows, "mlp", axis=1, tiled=True)
    model_width = x_full.shape[1]
    mixing = add_columns(
        x_full, lax.all_gather(w_fio.astype(jnp.bfloat16), "req", axis=0, tiled=True)
    )
    mixing = mixing.reshape(row_count, heads_here, 3, head_size)
    bias_table = forget_bias.reshape(heads_here, head_size)
    forget_logit = mixing[:, :, 0] + bias_table
    values = mixing[:, :, 1]
    queries = mixing[:, :, 2]
    prompt_forget = forget_logit[:prompt_rows].reshape(prompts_here, plen, heads_here, head_size)
    prompt_values = values[:prompt_rows].reshape(prompts_here, plen, heads_here, head_size)
    prompt_queries = queries[:prompt_rows].reshape(prompts_here, plen, heads_here, head_size)
    start_state = jnp.zeros((prompts_here, heads_here, head_size, head_size), jnp.float32)
    block_total = plen // BLOCK

    def to_blocks(source_array):
        return source_array.reshape(
            prompts_here, block_total, BLOCK, heads_here, head_size
        ).transpose(1, 0, 2, 3, 4)

    def scan_block(carried, inputs):
        forget_block, value_block, query_block, start_row = inputs
        return block_step(
            carried, forget_block, value_block, query_block, start_row, prompt_lengths
        )

    starts = jnp.arange(block_total, dtype=jnp.int32) * BLOCK
    prompt_states, block_outputs = lax.scan(
        scan_block,
        start_state,
        (to_blocks(prompt_forget), to_blocks(prompt_values), to_blocks(prompt_queries), starts),
    )
    prompt_mixed = block_outputs.transpose(1, 0, 2, 3, 4).reshape(
        prompts_here, plen, heads_here, head_size
    )
    decode_logit = forget_logit[prompt_rows:]
    decode_next = (
        jax.nn.sigmoid(decode_logit)[..., None] * decode_states
        + jax.nn.sigmoid(-decode_logit)[..., None] * values[prompt_rows:][:, :, None, :]
    )
    decode_mixed = jnp.einsum(
        "nhcv,nhc->nhv", decode_next, queries[prompt_rows:], precision=lax.Precision.HIGHEST
    )
    mixed_all = jnp.concatenate(
        [prompt_mixed.reshape(prompt_rows, heads_here, head_size), decode_mixed], axis=0
    )
    mean_square = jnp.mean(mixed_all * mixed_all, axis=-1, keepdims=True)
    head_rows = (
        mixed_all * lax.rsqrt(mean_square + epsilon) * head_gain.reshape(heads_here, head_size)
    ).astype(jnp.bfloat16)
    head_rows = head_rows.reshape(row_count, heads_here * head_size)
    offset = lax.axis_index("mlp") * feature_part
    head_terms = project_output(head_rows, w_out.astype(jnp.bfloat16))
    attention = lax.psum_scatter(
        head_terms.astype(jnp.bfloat16), "mlp", scatter_dimension=1, tiled=True
    ).astype(jnp.float32)
    residual = (local_rows.astype(jnp.float32) + attention).astype(jnp.bfloat16)
    residual_wide = residual.astype(jnp.float32)
    square_sum = lax.psum(jnp.sum(residual_wide * residual_wide, axis=1), "mlp")
    row_scale = lax.rsqrt(square_sum / model_width + epsilon)[:, None]
    gain_part = lax.dynamic_slice_in_dim(mlp_gain, offset, feature_part)
    normed_part = (residual_wide * row_scale * gain_part).astype(jnp.bfloat16)
    normed = lax.all_gather(normed_part, "mlp", axis=1, tiled=True)
    gate_up = add_columns(
        normed, lax.all_gather(w_gu.astype(jnp.bfloat16), "req", axis=0, tiled=True)
    )
    hidden_here = w_gu.shape[1] // 2
    hidden = (jax.nn.silu(gate_up[:, :hidden_here]) * gate_up[:, hidden_here:]).astype(jnp.bfloat16)
    down_terms = jnp.dot(
        hidden,
        lax.all_gather(w_down.astype(jnp.bfloat16), "req", axis=1, tiled=True),
        preferred_element_type=jnp.float32,
    )
    down_share = lax.psum_scatter(
        down_terms.astype(jnp.bfloat16), "mlp", scatter_dimension=1, tiled=True
    ).astype(jnp.float32)
    layer_output = (residual_wide + down_share).astype(jnp.bfloat16)
    prompt_out = layer_output[:prompt_rows].reshape(prompts_here, plen, feature_part)
    decode_out = layer_output[prompt_rows:]
    return (prompt_out, decode_out, prompt_states, decode_next)


def solution(mesh):
    placed = (
        P("req", None, "mlp"),
        P("req", "mlp"),
        P("req"),
        P("req", "mlp", None, None),
        P("req", "mlp"),
        P("mlp"),
        P("mlp"),
        P("mlp", "req"),
        P(),
        P("req", "mlp"),
        P("mlp", "req"),
    )
    return jax.shard_map(
        on_device,
        mesh=mesh,
        in_specs=placed,
        out_specs=(
            P("req", None, "mlp"),
            P("req", "mlp"),
            P("req", "mlp", None, None),
            P("req", "mlp", None, None),
        ),
        check_vma=False,
    )
```

profile of v0, /device:TPU:0, one launch (start us, length us, event | category | flops | bytes accessed | tf_op | source)
XLA Modules:
  0.0 637.0 jit_solution(2306237471951861111)
XLA Ops:
  7.2 1.8 convert_element_type.49
  9.1 1.5 pad_maximum_fusion
  10.7 38.0 %all_gather.20 = bf16[128,2048]{1,0:T(8,128)(2,1)} all-gather(bf16[128,256]{1,0:T(8,128)(2,1)S(1)} %convert_element_type.51), channel_id=1, replica_groups=mesh['req'=8,'mlp'=16] {'req'}, dimensions={1}, use_global_device_ids=true | all-gather | bytes 589824 | tf_op jit(solution)/shard_map/all_gather | solution.py:17
  48.7 17.3 %all-gather.8.cloned.1.call-done = bf16[2048,384]{1,0:T(8,128)(2,1)} async-done(((bf16[256,384]{1,0:T(8,128)(2,1)}), bf16[2048,384]{1,0:T(8,128)(2,1)}) %all-gather.8.cloned.1.call-update) | async-done | bytes 1572880 | tf_op jit(solution)/shard_map/all_gather | solution.py:71
  66.1 61.3 %all-gather.6.cloned.1.call-done = bf16[2052,2048]{1,0:T(8,128)(2,1)} async-done(((bf16[2052,128]{1,0:T(8,128)(2,1)}), bf16[2052,2048]{1,0:T(8,128)(2,1)}) %all-gather.6.cloned.1.call-update) | async-done | bytes 8405008 | tf_op jit(solution)/shard_map/all_gather | solution.py:68
  127.4 7.4 %fusion.59 = f32[2052,384]{0,1:T(8,128)S(1)} fusion(bf16[2052,2048]{1,0:T(8,128)(2,1)} %all-gather.6.cloned.1.call-done, bf16[2048,384]{1,0:T(8,128)(2,1)} %all-gather.8.cloned.1.call-done), kind=kOutput, calls=%fused_computation.84 | convolution fusion | flops 3227516928 | bytes 13129728 | tf_op jit(solution)/shard_map/dot_general | solution.py:11
  134.9 1.6 copy-done.3
  137.3 2.2 copy-done.4
  140.8 2.6 copy.47
  143.3 1.3 copy.48
  144.7 108.7 %while.13 = (s32[]{:T(128)}, f32[2,1,128,128]{3,2,0,1:T(8,128)S(1)}, f32[16,2,64,1,128]{4,2,0,1,3:T(8,128)}, s32[16]{0:T(128)S(1)}, s32[2]{0:T(128)S(1)}, /*inde...) while((s32[]{:T(128)}, ...), condition=%wide.region_2.3_spmd.clone, body=%wide.region_0.2_spmd.clone.sunk | while | flops 77050048 | bytes 1596940 | solution.py:96
  146.2 1.2 convolution_select_fusion.2
  148.4 1.7 fusion.93
  150.1 1.3 fusion.91
  152.9 1.2 convolution_select_fusion.2
  155.2 1.7 fusion.93
  156.9 1.3 fusion.91
  159.8 1.2 convolution_select_fusion.2
  162.0 1.7 fusion.93
  163.7 1.3 fusion.91
  166.6 1.2 convolution_select_fusion.2
  168.8 1.7 fusion.93
  170.5 1.3 fusion.91
  173.3 1.2 convolution_select_fusion.2
  175.6 1.7 fusion.93
  177.3 1.3 fusion.91
  180.1 1.2 convolution_select_fusion.2
  182.4 1.7 fusion.93
  184.1 1.3 fusion.91
  189.2 1.7 fusion.93
  190.9 1.3 fusion.91
  196.0 1.7 fusion.93
  197.7 1.3 fusion.91
  202.8 1.7 fusion.93
  204.5 1.3 fusion.91
  209.6 1.7 fusion.93
  211.3 1.3 fusion.91
  216.4 1.7 fusion.93
  218.1 1.3 fusion.91
  223.2 1.7 fusion.93
  224.9 1.3 fusion.91
  229.9 1.7 fusion.93
  231.7 1.3 fusion.91
  236.7 1.7 fusion.93
  238.5 1.3 fusion.91
  243.5 1.7 fusion.93
  245.3 1.3 fusion.91
  250.3 1.7 fusion.93
  252.1 1.3 fusion.91
  254.0 1.6 fusion.49
  255.7 5.6 convolution_convert_fusion.1
  261.3 11.6 %copy.58 = bf16[2052,2048]{0,1:T(8,128)(2,1)} copy(bf16[2052,2048]{1,0:T(8,128)(2,1)} %convolution_convert_fusion.1) | data formatting | bytes 16809984
  275.6 73.2 %reduce-scatter.7.cloned.1.call-done = bf16[128,2052]{1,0:T(8,128)(2,1)} async-done(((bf16[2048,2052]{1,0:T(8,128)(2,1)}), bf16[128,2052]{1,0:T(8,128)(2,1)}) %reduce-scatter.7.cloned.1.call-update) | async-done | bytes 525328
  348.8 1.3 copy.59
  350.5 54.1 %psum.7 = f32[2052]{0:T(1024)S(1)} all-reduce(f32[2052]{0:T(1024)S(1)} %fusion.43), channel_id=1, replica_groups=mesh['req'=8,'mlp'=16] {'mlp'}, use_global_device_ids=true, to_apply=%region_6.7 | all-reduce | flops 2052 | bytes 16416 | tf_op jit(solution)/shard_map/psum | solution.py:127
  404.7 1.2 fusion.45
  406.9 8.9 %all-gather.12.cloned.1.call-done = bf16[2048,704]{0,1:T(8,128)(2,1)} async-done(((bf16[256,704]{0,1:T(8,128)(2,1)}), bf16[2048,704]{0,1:T(8,128)(2,1)}) %all-gather.12.cloned.1.call-update) | async-done | bytes 2883600 | tf_op jit(solution)/shard_map/all_gather | solution.py:133
  415.8 60.6 %all-gather.10.cloned.1.call-done = bf16[2052,2048]{1,0:T(8,128)(2,1)} async-done(((bf16[2052,128]{1,0:T(8,128)(2,1)}), bf16[2052,2048]{1,0:T(8,128)(2,1)}) %all-gather.10.cloned.1.call-update) | async-done | bytes 8405008 | tf_op jit(solution)/shard_map/all_gather | solution.py:131
  476.4 12.6 %fusion.60 = f32[2052,704]{0,1:T(8,128)} fusion(bf16[2052,2048]{1,0:T(8,128)(2,1)} %all-gather.10.cloned.1.call-done, bf16[2048,704]{0,1:T(8,128)(2,1)} %all-gather.12.cloned.1.call-done), kind=kOutput, calls=%fused_computation.85 | convolution fusion | flops 5917114368 | bytes 17067008 | tf_op jit(solution)/shard_map/dot_general | solution.py:11
  489.0 41.2 %all-gather.14.cloned.1.call-done = bf16[352,2048]{1,0:T(8,128)(2,1)} async-done(((bf16[352,256]{1,0:T(8,128)(2,1)}), bf16[352,2048]{1,0:T(8,128)(2,1)}) %all-gather.14.cloned.1.call-update) | async-done | bytes 1441808 | tf_op jit(solution)/shard_map/all_gather | solution.py:139
  530.1 11.1 %convolution_convert_fusion = bf16[2052,2048]{1,0:T(8,128)(2,1)} fusion(bf16[352,2048]{1,0:T(8,128)(2,1)} %all-gather.14.cloned.1.call-done, f32[2052,704]{0,1:T(8,128)} %fusion.60), kind=kOutput, calls=%fused_computation.48 | convolution fusion | flops 2967093504 | bytes 15625216 | tf_op jit(solution)/shard_map/dot_general | solution.py:137
  541.2 11.5 %copy.60 = bf16[2052,2048]{0,1:T(8,128)(2,1)} copy(bf16[2052,2048]{1,0:T(8,128)(2,1)} %convolution_convert_fusion) | data formatting | bytes 16809984
  552.8 74.4 %reduce-scatter.9.cloned.1.call-done = bf16[128,2052]{1,0:T(8,128)(2,1)} async-done(((bf16[2048,2052]{1,0:T(8,128)(2,1)}), bf16[128,2052]{1,0:T(8,128)(2,1)}) %reduce-scatter.9.cloned.1.call-update) | async-done | bytes 525328
  627.2 1.3 copy.61
  (223 shorter events, 60.6 us)
Async XLA Ops:
  7.2 1.9 copy-start
  7.2 3.5 copy-start.11
  7.2 58.9 %all-gather.8.cloned.1.call-start = ((), (), s32[]{:S(2)}) async-start(), calls=%async_computation.3 | async-start | bytes 1769472 | tf_op jit(solution)/shard_map/all_gather | solution.py:71
  9.0 118.4 %all-gather.6.cloned.1.call-start = ((), (), s32[]{:S(2)}) async-start(), calls=%async_computation.2 | async-start | bytes 8947712 | tf_op jit(solution)/shard_map/all_gather | solution.py:68
  10.6 338.2 %reduce-scatter.7.cloned.1.call-start = ((), (), s32[]{:S(2)}) async-start(), calls=%async_computation.7 | async-start | bytes 9469952
  134.8 1.7 copy-start.3
  136.5 0.7 copy-start.14
  137.2 2.3 copy-start.4
  137.3 3.4 copy-start.1
  143.3 1.3 slice-start
  143.3 1.3 copy-start.15
  144.7 108.8 %copy-start.10 = (f32[4,1,128,128]{3,2,1,0:T(8,128)S(1)}, f32[4,1,128,128]{3,2,1,0:T(8,128)}, u32[]{:S(2)}) copy-start(f32[4,1,128,128]{3,2,1,0:T(8,128)} %param.16) | copy-start | bytes 786436
  253.4 7.9 %copy-start.5 = (f32[2,1,128,128]{3,2,0,1:T(8,128)}, f32[2,1,128,128]{3,2,0,1:T(8,128)S(1)}, u32[]{:S(2)}) copy-start(f32[2,1,128,128]{3,2,0,1:T(8,128)S(1)} %get-tuple-element.114) | copy-start | bytes 393220
  253.4 2.3 copy-start.2
  253.4 2.3 copy-start.6
  253.4 2.3 copy-start.13
  253.6 7.7 %copy-start.7 = (f32[4,1,128,128]{3,2,1,0:T(8,128)}, f32[4,1,128,128]{3,2,1,0:T(8,128)S(1)}, u32[]{:S(2)}) copy-start(f32[4,1,128,128]{3,2,1,0:T(8,128)S(1)} %multiply_add_fusion) | copy-start | bytes 786436
  272.9 1.1 copy-start.8
  272.9 77.2 %copy-start.12 = (bf16[4,128]{1,0:T(4,128)(2,1)S(1)}, bf16[4,128]{1,0:T(4,128)(2,1)}, u32[]{:S(2)}) copy-start(bf16[4,128]{1,0:T(4,128)(2,1)} %param.14) | copy-start | bytes 3076
  272.9 142.9 %all-gather.12.cloned.1.call-start = ((), (), s32[]{:S(2)}) async-start(), calls=%async_computation.5 | async-start | bytes 3244032 | tf_op jit(solution)/shard_map/all_gather | solution.py:133
  274.8 201.6 %all-gather.10.cloned.1.call-start = ((), (), s32[]{:S(2)}) async-start(), calls=%async_computation.4 | async-start | bytes 8947712 | tf_op jit(solution)/shard_map/all_gather | solution.py:131
  350.5 55.4 %copy-start.9 = (f32[352,256]{1,0:T(8,128)S(1)}, f32[352,256]{1,0:T(8,128)}, u32[]{:S(2)}) copy-start(f32[352,256]{1,0:T(8,128)} %param.23) | copy-start | bytes 1081348
  405.9 124.3 %all-gather.14.cloned.1.call-start = ((), (), s32[]{:S(2)}) async-start(), calls=%async_computation.6 | async-start | bytes 1622016 | tf_op jit(solution)/shard_map/all_gather | solution.py:139
  406.7 220.6 %reduce-scatter.9.cloned.1.call-start = ((), (), s32[]{:S(2)}) async-start(), calls=%async_computation.8 | async-start | bytes 9469952
Sparse Core Ops, SparseCore 0:
  10.9 55.1 all-gather.7
  67.7 59.6 all-gather.5
  273.0 75.7 reduce-scatter.6
  351.4 64.3 all-gather.11
  417.3 59.0 all-gather.9
  478.4 51.6 all-gather.13
  552.9 74.2 reduce-scatter.8
where the time goes:
time: 641 us; the launch traced here: 637 us
  waiting for transfers between devices  337 us (53%)
  matrix products  121 us (19%)
  blocking collectives  92.2 us (14%)
  local copies, waits for them, and re-layouts  48.2 us (8%)
  other arithmetic  22.7 us (4%)
  between operations  14.4 us (2%)
    unnamed x9, waiting for transfers between devices  148 us
    all_gather x1, waiting for transfers between devices, on_device(): x_full = lax.all_gather(local_rows, 'mlp', axis=1, tiled=True)  61.3 us
    all_gather x1, waiting for transfers between devices, on_device(): normed = lax.all_gather(normed_part, 'mlp', axis=1, tiled=True)  60.6 us
    psum x1, blocking collectives, on_device(): square_sum = lax.psum(jnp.sum(residual_wide * residual_wide, axis=1), 'mlp')  54.1 us
    all_gather x1, waiting for transfers between devices, on_device(): lax.all_gather(w_down.astype(jnp.bfloat16), 'req', axis=1, tiled=True)  41.2 us
    all_gather x1, blocking collectives, project_output(): lax.all_gather(weights, 'req', axis=1, tiled=True)  38 us
    unnamed x37, local copies, waits for them, and re-layouts  31.3 us
    dot_general x16, matrix products, block_step(): jnp.einsum('pthc,phcv->pthv', query_tilde, carried, precision=lax.Precisi...  27.6 us
  transfers between devices with their start and end apart: 7, of which 7 were waited for; matrix products, arithmetic and copies ran while one was open for 3% of the time, Pallas kernels for 0%

commit v1 on v0

--- a/solution.py
+++ b/solution.py
@@ -65,7 +65,9 @@
         [prompt_tokens.reshape(prompt_rows, feature_part), decode_tokens], axis=0
     )
     row_count = local_rows.shape[0]
-    x_full = lax.all_gather(local_rows, "mlp", axis=1, tiled=True)
+    x_full = jnp.concatenate(
+        lax.all_to_all(jnp.stack([local_rows] * lax.axis_size("mlp")), "mlp", 0, 0), axis=1
+    )
     model_width = x_full.shape[1]
     mixing = add_columns(
         x_full, lax.all_gather(w_fio.astype(jnp.bfloat16), "req", axis=0, tiled=True)

time: 641 us -> 672 us (1.048)
  blocking collectives: 92.2 us -> 185 us
  waiting for transfers between devices: 337 us -> 255 us
  local copies, waits for them, and re-layouts: 48.2 us -> 74.6 us
  matrix products: 121 us -> 110 us
    all_gather x1, blocking collectives: 38 us -> 131 us  [project_output(): lax.all_gather(weights, 'req', axis=1, tiled=True)]
    all_gather x1 -> x0, waiting for transfers between devices: 61.3 us -> none  [on_device(): x_full = lax.all_gather(local_rows, 'mlp', axis=1, tiled=True)]
    reshape x0 -> x2, local copies, waits for them, and re-layouts: none -> 27.8 us  [on_device(): jnp.concatenate(lax.all_to_all(jnp.stack([local_rows] * lax.axis_size('ml...]
    all_gather x1, waiting for transfers between devices: 17.3 us -> 0.01 us  [on_device(): lax.all_gather(w_fio.astype(jnp.bfloat16), 'req', axis=0, tiled=True)]
    dot_general x16, matrix products: 27.6 us -> 17.5 us  [block_step(): jnp.einsum('pthc,phcv->pthv', query_tilde, carried, precision=lax.Precisi...]
    unnamed x37 -> x28, local copies, waits for them, and re-layouts: 31.3 us -> 27.4 us
    unnamed x9 -> x8, waiting for transfers between devices: 148 us -> 144 us
  transfers between devices with their start and end apart: 7 -> 7, of which waited for: 7 -> 5; matrix products, arithmetic and copies ran while one was open for 3% -> 3% of each run, Pallas kernels for 0% -> 0%
where the time goes in v1:
time: 672 us; the launch traced here: 667 us
  waiting for transfers between devices  255 us (38%)
  blocking collectives  185 us (28%)
  matrix products  110 us (16%)
  local copies, waits for them, and re-layouts  74.6 us (11%)
  other arithmetic  20 us (3%)
  between operations  14.4 us (2%)
    unnamed x8, waiting for transfers between devices  144 us
    all_gather x1, blocking collectives, project_output(): lax.all_gather(weights, 'req', axis=1, tiled=True)  131 us
    all_gather x1, waiting for transfers between devices, on_device(): normed = lax.all_gather(normed_part, 'mlp', axis=1, tiled=True)  60.5 us
    psum x1, blocking collectives, on_device(): square_sum = lax.psum(jnp.sum(residual_wide * residual_wide, axis=1), 'mlp')  54 us
    all_gather x1, waiting for transfers between devices, on_device(): lax.all_gather(w_down.astype(jnp.bfloat16), 'req', axis=1, tiled=True)  41.1 us
    reshape x2, local copies, waits for them, and re-layouts, on_device(): jnp.concatenate(lax.all_to_all(jnp.stack([local_rows] * lax.axis_size('ml...  27.8 us
    unnamed x28, local copies, waits for them, and re-layouts  27.4 us
    dot_general x16, matrix products, block_step(): jnp.einsum('pthc,pthv->phcv', key_decayed, value_block, precision=lax.Pre...  21 us
  transfers between devices with their start and end apart: 7, of which 5 were waited for; matrix products, arithmetic and copies ran while one was open for 3% of the time, Pallas kernels for 0%

profile of v1, /device:TPU:0, one launch (start us, length us, event | category | flops | bytes accessed | tf_op | source)
XLA Modules:
  0.0 667.3 jit_solution(323254812539026938)
XLA Ops:
  8.3 4.3 stack.2
  12.6 6.0 all-to-all-start
  19.5 131.1 %all_gather.16 = bf16[128,2048]{1,0:T(8,128)(2,1)S(1)} all-gather(bf16[128,256]{1,0:T(8,128)(2,1)S(1)} %convert_element_type.51), channel_id=1, replica_groups=mesh['req'=8,'mlp'=16] {'req'}, dimensions={1}, use_global_device_ids=true | all-gather | bytes 589824 | tf_op jit(solution)/shard_map/all_gather | solution.py:17
  150.6 1.7 copy.31
  152.4 14.3 %copy.30 = bf16[2052,16,128]{2,1,0:T(8,128)(2,1)} copy(bf16[2052,16,128]{2,0,1:T(8,128)(2,1)} %bitcast.1) | data formatting | bytes 16809984 | tf_op jit(solution)/shard_map/reshape | solution.py:68
  166.7 13.5 %reshape.334 = bf16[2052,2048,1]{1,0,2:T(8,128)(2,1)} reshape(bf16[2052,16,128]{2,1,0:T(8,128)(2,1)} %copy.30) | data formatting | bytes 16809984 | tf_op jit(solution)/shard_map/reshape | solution.py:68
  180.1 7.0 %convolution_bitcast_fusion.2 = f32[2052,1,3,128]{3,0,2,1:T(8,128)S(1)} fusion(bf16[2052,2048,1]{1,0,2:T(8,128)(2,1)} %reshape.334, bf16[3,128,2048]{2,1,0:T(8,128)(2,1)S(1)} %bitcast.183), kind=kOutput, calls=%fused_computation.50 | convolution fusion | flops 3227516928 | bytes 13129728 | tf_op jit(solution)/shard_map/dot_general | solution.py:11
  188.1 1.5 copy_bitcast_fusion
  189.6 98.8 %while.13 = (s32[]{:T(128)}, f32[2,1,128,128]{3,2,0,1:T(8,128)S(1)}, f32[16,2,64,1,128]{4,2,0,1,3:T(8,128)S(1)}, s32[16]{0:T(128)S(1)}, s32[2]{0:T(128)S(1)}, /*...) while((s32[]{:T(128)}, ...), condition=%wide.region_2.3_spmd.clone, body=%wide.region_0.2_spmd.clone.sunk | while | flops 77050048 | bytes 1597324 | solution.py:98
  191.1 1.1 convolution_select_fusion.2
  193.3 1.1 fusion.90
  194.4 1.3 fusion.88
  197.2 1.1 convolution_select_fusion.2
  199.4 1.1 fusion.90
  200.6 1.3 fusion.88
  203.4 1.1 convolution_select_fusion.2
  205.6 1.1 fusion.90
  206.7 1.3 fusion.88
  209.6 1.1 convolution_select_fusion.2
  211.8 1.1 fusion.90
  212.9 1.3 fusion.88
  215.8 1.1 convolution_select_fusion.2
  218.0 1.1 fusion.90
  219.1 1.3 fusion.88
  221.9 1.1 convolution_select_fusion.2
  224.1 1.1 fusion.90
  225.3 1.3 fusion.88
  228.1 1.1 convolution_select_fusion.2
  230.3 1.1 fusion.90
  231.5 1.3 fusion.88
  234.3 1.1 convolution_select_fusion.2
  236.5 1.1 fusion.90
  237.6 1.3 fusion.88
  240.5 1.1 convolution_select_fusion.2
  243.8 1.3 fusion.88
  246.6 1.1 convolution_select_fusion.2
  250.0 1.3 fusion.88
  252.8 1.1 convolution_select_fusion.2
  256.2 1.3 fusion.88
  259.0 1.1 convolution_select_fusion.2
  262.3 1.3 fusion.88
  265.2 1.1 convolution_select_fusion.2
  268.5 1.3 fusion.88
  271.3 1.1 convolution_select_fusion.2
  274.7 1.3 fusion.88
  277.5 1.1 convolution_select_fusion.2
  279.7 1.1 fusion.90
  280.9 1.3 fusion.88
  283.7 1.1 convolution_select_fusion.2
  287.0 1.3 fusion.88
  289.4 5.6 convolution_convert_fusion.1
  295.0 11.6 %copy.39 = bf16[2052,2048]{0,1:T(8,128)(2,1)} copy(bf16[2052,2048]{1,0:T(8,128)(2,1)} %convolution_convert_fusion.1) | data formatting | bytes 16809984
  309.3 69.8 %reduce-scatter.7.cloned.1.call-done = bf16[128,2052]{1,0:T(8,128)(2,1)} async-done(((bf16[2048,2052]{1,0:T(8,128)(2,1)}), bf16[128,2052]{1,0:T(8,128)(2,1)}) %reduce-scatter.7.cloned.1.call-update) | async-done | bytes 525328
  379.1 1.3 copy.40
  380.8 54.0 %psum.7 = f32[2052]{0:T(1024)S(1)} all-reduce(f32[2052]{0:T(1024)S(1)} %fusion.40), channel_id=1, replica_groups=mesh['req'=8,'mlp'=16] {'mlp'}, use_global_device_ids=true, to_apply=%region_6.7 | all-reduce | flops 2052 | bytes 16416 | tf_op jit(solution)/shard_map/psum | solution.py:129
  434.9 1.2 fusion.42
  437.1 9.0 %all-gather.9.cloned.1.call-done = bf16[2048,704]{0,1:T(8,128)(2,1)} async-done(((bf16[256,704]{0,1:T(8,128)(2,1)}), bf16[2048,704]{0,1:T(8,128)(2,1)}) %all-gather.9.cloned.1.call-update) | async-done | bytes 2883600 | tf_op jit(solution)/shard_map/all_gather | solution.py:135
  446.1 60.5 %all-gather.7.cloned.1.call-done = bf16[2052,2048]{1,0:T(8,128)(2,1)} async-done(((bf16[2052,128]{1,0:T(8,128)(2,1)}), bf16[2052,2048]{1,0:T(8,128)(2,1)}) %all-gather.7.cloned.1.call-update) | async-done | bytes 8405008 | tf_op jit(solution)/shard_map/all_gather | solution.py:133
  506.6 12.6 %fusion.57 = f32[2052,704]{0,1:T(8,128)} fusion(bf16[2052,2048]{1,0:T(8,128)(2,1)} %all-gather.7.cloned.1.call-done, bf16[2048,704]{0,1:T(8,128)(2,1)} %all-gather.9.cloned.1.call-done), kind=kOutput, calls=%fused_computation.88 | convolution fusion | flops 5917114368 | bytes 17067008 | tf_op jit(solution)/shard_map/dot_general | solution.py:11
  519.2 41.1 %all-gather.11.cloned.1.call-done = bf16[352,2048]{1,0:T(8,128)(2,1)} async-done(((bf16[352,256]{1,0:T(8,128)(2,1)}), bf16[352,2048]{1,0:T(8,128)(2,1)}) %all-gather.11.cloned.1.call-update) | async-done | bytes 1441808 | tf_op jit(solution)/shard_map/all_gather | solution.py:141
  560.3 11.1 %convolution_convert_fusion = bf16[2052,2048]{1,0:T(8,128)(2,1)} fusion(bf16[352,2048]{1,0:T(8,128)(2,1)} %all-gather.11.cloned.1.call-done, f32[2052,704]{0,1:T(8,128)} %fusion.57), kind=kOutput, calls=%fused_computation.48 | convolution fusion | flops 2967093504 | bytes 15625216 | tf_op jit(solution)/shard_map/dot_general | solution.py:139
  571.4 11.5 %copy.41 = bf16[2052,2048]{0,1:T(8,128)(2,1)} copy(bf16[2052,2048]{1,0:T(8,128)(2,1)} %convolution_convert_fusion) | data formatting | bytes 16809984
  583.0 74.5 %reduce-scatter.9.cloned.1.call-done = bf16[128,2052]{1,0:T(8,128)(2,1)} async-done(((bf16[2048,2052]{1,0:T(8,128)(2,1)}), bf16[128,2052]{1,0:T(8,128)(2,1)}) %reduce-scatter.9.cloned.1.call-update) | async-done | bytes 525328
  657.5 1.3 copy.42
  (213 shorter events, 57.6 us)
Async XLA Ops:
  12.6 6.1 copy-start.4
  12.6 6.9 %copy-start.7 = (f32[128,256]{1,0:T(8,128)S(1)}, f32[128,256]{1,0:T(8,128)}, u32[]{:S(2)}) copy-start(f32[128,256]{1,0:T(8,128)} %param.20) | copy-start | bytes 393220
  12.6 139.8 %all-to-all-start = ((bf16[16,2052,128]{2,1,0:T(8,128)(2,1)}), bf16[16,2052,128]{2,1,0:T(8,128)(2,1)}, u32[]{:S(2)}, u32[]{:S(2)}) async-start(bf16[16,2052,128]{2,1,0:T(8,128)(2,1)} %stack.2), calls=%async_computation | async-start | bytes 16842752 | tf_op jit(solution)/shard_map/all_to_all | solution.py:69
  18.6 132.0 %all-gather.5.cloned.1.call-start = ((), (), s32[]{:S(2)}) async-start(), calls=%async_computation.3 | async-start | bytes 1769472 | tf_op jit(solution)/shard_map/all_gather | solution.py:73
  19.4 359.7 %reduce-scatter.7.cloned.1.call-start = ((), (), s32[]{:S(2)}) async-start(), calls=%async_computation.7 | async-start | bytes 9469952
  187.1 0.7 copy-start.10
  188.1 1.5 copy-start.11
  189.5 98.8 %copy-start.6 = (f32[4,1,128,128]{3,2,1,0:T(8,128)S(1)}, f32[4,1,128,128]{3,2,1,0:T(8,128)}, u32[]{:S(2)}) copy-start(f32[4,1,128,128]{3,2,1,0:T(8,128)} %param.16) | copy-start | bytes 786436
  288.4 6.6 copy-start.1
  288.4 1.0 copy-start.9
  288.6 6.4 copy-start.2
  306.6 1.1 copy-start.3
  306.6 73.8 %copy-start = (bf16[2,1024,128]{2,1,0:T(8,128)(2,1)S(1)}, bf16[2,1024,128]{2,1,0:T(8,128)(2,1)}, u32[]{:S(2)}) copy-start(bf16[2,1024,128]{2,1,0:T(8,128)(2,1)} %param.13) | copy-start | bytes 1572868
  306.7 73.8 %copy-start.8 = (bf16[4,128]{1,0:T(4,128)(2,1)S(1)}, bf16[4,128]{1,0:T(4,128)(2,1)}, u32[]{:S(2)}) copy-start(bf16[4,128]{1,0:T(4,128)(2,1)} %param.14) | copy-start | bytes 3076
  306.7 139.4 %all-gather.9.cloned.1.call-start = ((), (), s32[]{:S(2)}) async-start(), calls=%async_computation.5 | async-start | bytes 3244032 | tf_op jit(solution)/shard_map/all_gather | solution.py:135
  308.5 198.0 %all-gather.7.cloned.1.call-start = ((), (), s32[]{:S(2)}) async-start(), calls=%async_computation.4 | async-start | bytes 8947712 | tf_op jit(solution)/shard_map/all_gather | solution.py:133
  380.5 55.7 %copy-start.5 = (f32[352,256]{1,0:T(8,128)S(1)}, f32[352,256]{1,0:T(8,128)}, u32[]{:S(2)}) copy-start(f32[352,256]{1,0:T(8,128)} %param.23) | copy-start | bytes 1081348
  436.1 124.3 %all-gather.11.cloned.1.call-start = ((), (), s32[]{:S(2)}) async-start(), calls=%async_computation.6 | async-start | bytes 1622016 | tf_op jit(solution)/shard_map/all_gather | solution.py:141
  436.9 220.7 %reduce-scatter.9.cloned.1.call-start = ((), (), s32[]{:S(2)}) async-start(), calls=%async_computation.8 | async-start | bytes 9469952
Sparse Core Ops, SparseCore 0:
  22.3 113.4 all-gather.4
  306.8 72.2 reduce-scatter.6
  381.9 64.1 all-gather.8
  447.5 58.9 all-gather.6
  508.6 51.6 all-gather.10
  583.1 74.3 reduce-scatter.8
